TPU v7x, 32 devices: a whole 2x2x4 slice. The times are simulated.
32 devices in a mesh: fsdp: 16 (over z, y, core), frame: 2 (over x).
Axes of the slice: x: 2, y: 2, z: 4, core: 2. Of those that a mesh axis runs over, the one named last changes fastest.
Arguments:
- student_tokens: bfloat16 [16, 8, 256, 3200], P('fsdp', 'frame'), may hold values from -6 to 6
- norm_gain: float32 [3200], replicated, may hold values from 0.1 to 1.9
- mae_weight: bfloat16 [3200, 1408], P('fsdp'), may hold values from -0.109375 to 0.109375
- clip_target: bfloat16 [16, 8, 3200], P('fsdp', 'frame'), may hold values from -6 to 6
- mae_target: bfloat16 [16, 8, 128, 1408], P('fsdp', 'frame'), may hold values from -6 to 6
- keep_mask: int32 [16, 8, 256], P('fsdp', 'frame'), may hold values 0 or 1
- teacher_gate: int32 [16], P('fsdp'), may hold values from 0 to 2
- temp_bucket: int32 [16], P('fsdp'), may hold values from 0 to 3
Outputs:
- token_grad: bfloat16 [16, 8, 256, 3200], P('fsdp', 'frame')
- weight_grad: float32 [3200, 1408], P('fsdp')
- gain_grad: float32 [3200], replicated
- loss: float32 [], replicated
Inputs may be any that keep to these rules, and one draw needn't show every extreme that they name: `teacher_gate`: 0 aligns a clip to both teachers, 1 to InternVL only, 2 to VideoMAE-g only.
All inputs are finite; a program needn't handle non-finite values. No bound on the sum of `keep_mask` on one device may be relied on, other than what follows from the above.
Results may differ from a plain program's by a relative error of at most 0.011.
Values may be sent and summed in bfloat16 or wider, within the bound.
A program may use at most 128 MiB of HBM per device.

v0:
```python
import jax
import jax.numpy as jnp
from jax import lax
from jax.sharding import PartitionSpec as P

epsilon = 1e-06


def swapped(shard, axis, stride):
    return lax.ppermute(shard, axis, [(i, i ^ 1 << stride) for i in range(lax.axis_size(axis))])


def unit_rows(values):
    inverse = lax.rsqrt(jnp.mean(values * values, axis=-1, keepdims=True) + epsilon)
    return (values * inverse, inverse)


def unit_grad(errors, unit, inverse):
    return inverse * (errors - unit * jnp.mean(errors * unit, axis=-1, keepdims=True))


def over_rows(left, right):
    return lax.dot_general(
        left, right, (((0,), (0,)), ((), ())), preferred_element_type=jnp.float32
    )


def back_project(grads, weight):
    return (
        0.5
        * lax.dot_general(
            grads, weight, (((1,), (1,)), ((), ())), preferred_element_type=jnp.float32
        )
    ).astype(jnp.bfloat16)


def per_device(
    student_tokens,
    norm_gain,
    mae_weight,
    clip_target,
    mae_target,
    keep_mask,
    teacher_gate,
    temp_bucket,
):
    samples, frames_here, patches, model_width = student_tokens.shape
    half_rows = patches // 2
    channels = mae_weight.shape[1]
    frame_devices = lax.axis_size("frame")
    top_bit = frame_devices.bit_length() - 2
    weight = lax.all_gather(mae_weight, "fsdp", axis=0, tiled=True)
    token_float = student_tokens.astype(jnp.float32)
    recip = lax.rsqrt(jnp.mean(token_float * token_float, axis=-1, keepdims=True) + epsilon)
    normed = (token_float * recip * norm_gain).astype(jnp.bfloat16)
    keep_float = keep_mask.astype(jnp.float32)
    pooled = (
        jnp.einsum(
            "bfp,bfpd->bfd",
            keep_mask.astype(jnp.bfloat16),
            normed,
            preferred_element_type=jnp.float32,
        )
        / patches
    )
    clip_unit, clip_inverse = unit_rows(pooled)
    teach_unit, unused_one = unit_rows(clip_target.astype(jnp.float32))
    clip_err = clip_unit - teach_unit
    clip_loss = 0.5 * jnp.sum(clip_err * clip_err, axis=-1)
    scaling = jnp.exp2(temp_bucket.astype(jnp.float32))
    clip_on = (teacher_gate != 2).astype(jnp.float32)
    mae_on = (teacher_gate != 1).astype(jnp.float32)
    parity = lax.axis_index("frame") // (frame_devices // 2)
    halves = normed.reshape(samples, frames_here, 2, half_rows, model_width)
    mask_halves = keep_mask.astype(jnp.bfloat16).reshape(samples, frames_here, 2, half_rows)
    own_half = lax.dynamic_slice_in_dim(halves, parity, 1, 2)[:, :, 0]
    sent_half = lax.dynamic_slice_in_dim(halves, 1 - parity, 1, 2)[:, :, 0]
    own_mask = lax.dynamic_slice_in_dim(mask_halves, parity, 1, 2)[:, :, 0]
    sent_mask = lax.dynamic_slice_in_dim(mask_halves, 1 - parity, 1, 2)[:, :, 0]
    got_half, got_mask = swapped((sent_half, sent_mask), "frame", top_bit)
    first_rows = own_half.reshape(-1, model_width)
    second_rows = got_half.reshape(-1, model_width)
    live = (own_mask.astype(jnp.float32) * got_mask.astype(jnp.float32)).reshape(samples, -1)
    projected = 0.5 * (
        jnp.dot(first_rows, weight, preferred_element_type=jnp.float32)
        + jnp.dot(second_rows, weight, preferred_element_type=jnp.float32)
    )
    proj_unit, proj_inverse = unit_rows(projected)
    target_unit, unused_two = unit_rows(mae_target.reshape(-1, channels).astype(jnp.float32))
    mae_err = proj_unit - target_unit
    mae_loss = (0.5 * jnp.sum(mae_err * mae_err, axis=-1)).reshape(samples, -1)
    sample_loss = scaling * (
        clip_on * jnp.sum(clip_loss, axis=1) + mae_on * jnp.sum(live * mae_loss, axis=1)
    )
    row_scale = ((scaling * mae_on)[:, None] * live).reshape(-1)
    row_grad = (row_scale[:, None] * unit_grad(mae_err, proj_unit, proj_inverse)).astype(
        jnp.bfloat16
    )
    shard = lax.psum_scatter(
        0.5 * (over_rows(first_rows, row_grad) + over_rows(second_rows, row_grad)),
        "fsdp",
        scatter_dimension=0,
        tiled=True,
    )
    shard = lax.psum_scatter(shard, "frame", scatter_dimension=1, tiled=True)
    shard = lax.all_gather(shard, "frame", axis=1, tiled=True)
    clip_count = samples * lax.axis_size("fsdp")
    weight_grad = shard / clip_count
    pair_grad = back_project(row_grad, weight).reshape(samples, frames_here, half_rows, model_width)
    returned = swapped(pair_grad, "frame", top_bit)
    lower_first = jnp.stack([pair_grad, returned], axis=2)
    upper_first = jnp.stack([returned, pair_grad], axis=2)
    spread = jnp.where(parity == 0, lower_first, upper_first)
    spread = spread.reshape(samples, frames_here, patches, model_width).astype(jnp.float32)
    clip_grad = (scaling * clip_on)[:, None, None] * unit_grad(clip_err, clip_unit, clip_inverse)
    normed_grad = spread + keep_float[:, :, :, None] * clip_grad[:, :, None, :] / patches
    inner = jnp.mean(normed_grad * norm_gain * token_float, axis=-1, keepdims=True)
    token_grad = (recip * (norm_gain * normed_grad - token_float * recip * recip * inner)).astype(
        jnp.bfloat16
    )
    gain_local = jnp.sum(normed_grad * token_float * recip, axis=(0, 1, 2))
    loss_local = jnp.sum(sample_loss)
    gain_total, loss_total = lax.psum((gain_local, loss_local), ("fsdp", "frame"))
    frame_count = frames_here * frame_devices
    gain_grad = gain_total / clip_count
    loss = loss_total / (clip_count * frame_count * patches * channels)
    return (token_grad, weight_grad, gain_grad, loss)


def solution(mesh):
    placed = (
        P("fsdp", "frame", None, None),
        P(),
        P("fsdp", None),
        P("fsdp", "frame", None),
        P("fsdp", "frame", None, None),
        P("fsdp", "frame", None),
        P("fsdp"),
        P("fsdp"),
    )
    return jax.shard_map(
        per_device,
        mesh=mesh,
        in_specs=placed,
        out_specs=(P("fsdp", "frame", None, None), P("fsdp", None), P(), P()),
        check_vma=False,
    )
```

profile of v0, /device:TPU:0, one launch (start us, length us, event | category | flops | bytes accessed | tf_op | source)
XLA Modules:
  0.0 434.5 jit_solution(7674785082313607338)
XLA Ops:
  8.0 4.4 %fusion.7 = f32[4,256]{1,0:T(4,128)S(1)} fusion(bf16[1,4,256,3200]{3,2,1,0:T(8,128)(2,1)} %param.8), kind=kLoop, calls=%fused_computation.12 | loop fusion | flops 9829376 | bytes 6557696 | tf_op jit(solution)/shard_map/reduce_sum | solution.py:54
  12.7 2.6 fusion.2
  15.3 3.2 dynamic-slice_bitcast_fusion
  18.6 1.7 copy-done.1
  20.2 3.2 collective-permute-start.1
  25.3 65.8 %all-gather.4.cloned.1.call-done = bf16[3200,1408]{1,0:T(8,128)(2,1)} async-done(((bf16[200,1408]{1,0:T(8,128)(2,1)}), bf16[3200,1408]{1,0:T(8,128)(2,1)}) %all-gather.4.cloned.1.call-update) | async-done | bytes 9011216 | tf_op jit(solution)/shard_map/all_gather | solution.py:52
  91.1 9.5 %fusion.26 = f32[512,1408]{1,0:T(8,128)S(1)} fusion(bf16[512,3200]{1,0:T(8,128)(2,1)} %bitcast.116, bf16[3200,1408]{1,0:T(8,128)(2,1)} %all-gather.4.cloned.1.call-done), kind=kOutput, calls=%fused_computation.71 | convolution fusion | flops 4613734400 | bytes 15171584 | tf_op jit(solution)/shard_map/dot_general | solution.py:85
  100.7 7.5 %multiply_reduce_fusion.3 = (f32[512]{0:T(512)S(1)}, f32[512,1408]{1,0:T(8,128)S(1)}) fusion(f32[512,1408]{1,0:T(8,128)S(1)} %fusion.26, bf16[512,3200]{1,0:T(8,128)(2,1)} %bitcast.8, bf16[3200,1408]{1,0:T(8,128)(2,1)S(1)} %copy-done.7), kind=kOutput, calls=%fused_computation.31 | convolution fusion | flops 4616617472 | bytes 18057216 | tf_op jit(solution)/shard_map/dot_general | solution.py:86
  110.8 9.1 %fusion.27 = f32[3200,1408]{1,0:T(8,128)} fusion(bf16[512,3200]{1,0:T(8,128)(2,1)S(1)} %bitcast.117, bf16[512,1408]{1,0:T(8,128)(2,1)S(1)} %multiply_convert_fusion), kind=kOutput, calls=%fused_computation.72 | convolution fusion | flops 4613734400 | bytes 22740992 | tf_op jit(solution)/shard_map/dot_general | solution.py:23
  119.9 13.7 %add_multiply_fusion = f32[3200,1408]{1,0:T(8,128)} fusion(f32[3200,1408]{1,0:T(8,128)} %fusion.27, bf16[512,3200]{1,0:T(8,128)(2,1)} %bitcast.8, bf16[512,1408]{1,0:T(8,128)(2,1)S(1)} %multiply_convert_fusion), kind=kOutput, calls=%fused_computation.4 | convolution fusion | flops 4622745600 | bytes 40763392 | tf_op jit(solution)/shard_map/dot_general | solution.py:23
  133.7 10.6 %fusion.14 = bf16[512,3200]{1,0:T(8,128)(2,1)} fusion(bf16[512,1408]{1,0:T(8,128)(2,1)S(1)} %multiply_convert_fusion, bf16[3200,1408]{1,0:T(8,128)(2,1)} %all-gather.4.cloned.1.call-done), kind=kOutput, calls=%fused_computation.22 | convolution fusion | flops 4617011200 | bytes 13729792 | tf_op jit(solution)/shard_map/dot_general | solution.py:31
  144.3 1.5 collective-permute-start.2
  145.9 5.0 %fusion.12 = f32[4,1,3200]{2,1,0:T(1,128)S(1)} fusion(bf16[1,4,256,3200]{3,2,1,0:T(8,128)(2,1)} %copy-done.1, bf16[4,256,1]{1,0,2:T(4,128)(2,1)S(1)} %get-tuple-element.15), kind=kOutput, calls=%fused_computation.20 | convolution fusion | flops 6553600 | bytes 6606848 | tf_op jit(solution)/shard_map/bfp,bfpd->bfd/dot_general | solution.py:58
  153.3 170.9 %reduce-scatter.9.cloned.1.call-done = f32[200,1408]{1,0:T(8,128)} async-done(((f32[3200,1408]{1,0:T(8,128)}), f32[200,1408]{1,0:T(8,128)}) %reduce-scatter.9.cloned.1.call-update) | async-done | bytes 1126416
  324.2 2.8 copy.19
  327.1 8.7 %fusion.11 = f32[1,4,2,128,3200]{4,3,1,2,0:T(8,128)} fusion(bf16[1,4,1,128,3200]{4,3,1,2,0:T(8,128)(2,1)S(1)} %bitcast.118, bf16[1,4,1,128,3200]{4,3,1,2,0:T(8,128)(2,1)} %bitcast.11, pred[]{:T(512)S(6)} %eq.3), kind=kLoop, calls=%fused_computation.19 | loop fusion | flops 13107200 | bytes 19660800 | tf_op jit(solution)/shard_map/convert_element_type | solution.py:114
  335.8 10.4 %copy.15 = f32[1,4,2,128,3200]{4,3,2,1,0:T(8,128)} copy(f32[1,4,2,128,3200]{4,3,1,2,0:T(8,128)} %fusion.11) | data formatting | bytes 26214400 | tf_op jit(solution)/shard_map/convert_element_type | solution.py:114
  346.2 9.5 %fusion.10 = (f32[3200]{0:T(1024)S(1)}, f32[4,256]{1,0:T(4,128)S(1)}) fusion(bf16[1,4,256,3200]{3,2,1,0:T(8,128)(2,1)} %param.8, f32[1,4,2,128,3200]{4,3,2,1,0:T(8,128)} %copy.15, f32[4,3200]{1,0:T(4,128)S(1)} %fusion.20, f32[4,256]{1,0:T(4,128)S(1)} %get-tuple-element.14, f32[4,256]{1,0:T(4,128)S(1)} %add_rsqrt_fusion, f32[3200]{0:T(1024)S(1)} %copy-done.5), kind=kLoop, calls=%fused_computation.15 | loop fusion | flops 32763776 | bytes 19749888 | tf_op jit(solution)/shard_map/reduce_sum | solution.py:121
  355.7 40.4 %all-reduce.1 = (f32[3200]{0:T(1024)S(1)}, f32[]{:T(128)}) all-reduce(f32[3200]{0:T(1024)S(1)} %get-tuple-element.4, f32[]{:T(128)} %bitcast.30), channel_id=1, replica_groups=mesh['fsdp'=16,'frame'=2] {'fsdp','frame'}, use_global_device_ids=true, to_apply=%region_11.12 | all-reduce | flops 3201 | bytes 25608 | tf_op jit(solution)/shard_map/psum | solution.py:123
  397.3 2.2 copy.20
  399.5 12.0 %fusion.6 = bf16[1,4,256,3200]{3,2,1,0:T(8,128)(2,1)} fusion(bf16[1,4,256,3200]{3,2,1,0:T(8,128)(2,1)} %param.8, f32[1,4,2,128,3200]{4,3,2,1,0:T(8,128)} %copy.15, f32[4,256]{1,0:T(4,128)S(1)} %broadcast_multiply_fusion.2, f32[4,3200]{1,0:T(4,128)S(1)} %fusion.20, f32[4,256]{1,0:T(4,128)S(1)} %get-tuple-element.14, f32[3200]{0:T(1024)S(1)} %copy-done.5, ...), kind=kLoop, calls=%fused_computation.11 | loop fusion | flops 36044800 | bytes 26290688 | tf_op jit(solution)/shard_map/convert_element_type | solution.py:118
  411.6 11.2 %all-gather.6.cloned.1.call-done = f32[2,704,200]{1,2,0:T(8,128)} async-done(((f32[1,704,200]{1,2,0:T(8,128)}), f32[2,704,200]{1,2,0:T(8,128)}) %all-gather.6.cloned.1.call-update) | async-done | bytes 1126416 | tf_op jit(solution)/shard_map/all_gather | solution.py:106
  422.8 1.4 broadcast_multiply_fusion
  424.8 2.0 reshape.268
  (49 shorter events, 6.9 us)
Async XLA Ops:
  7.2 5.2 %copy-start.5 = (f32[3200]{0:T(1024)S(1)}, f32[3200]{0:T(1024)}, u32[]{:S(2)}) copy-start(f32[3200]{0:T(1024)} %param.9) | copy-start | bytes 38404
  7.2 83.9 %all-gather.4.cloned.1.call-start = ((), (), s32[]{:S(2)}) async-start(), calls=%async_computation.2 | async-start | bytes 9574400 | tf_op jit(solution)/shard_map/all_gather | solution.py:52
  7.9 316.3 %reduce-scatter.9.cloned.1.call-start = ((), (), s32[]{:S(2)}) async-start(), calls=%async_computation.5 | async-start | bytes 19148800
  8.0 4.7 %copy-start = (bf16[1,4,256,3200]{3,2,1,0:T(8,128)(2,1)S(1)}, bf16[1,4,256,3200]{3,2,1,0:T(8,128)(2,1)}, u32[]{:S(2)}) copy-start(bf16[1,4,256,3200]{3,2,1,0:T(8,128)(2,1)} %param.8) | copy-start | bytes 19660804
  15.3 4.9 %copy-start.1 = (bf16[1,4,256,3200]{3,2,1,0:T(8,128)(2,1)}, bf16[1,4,256,3200]{3,2,1,0:T(8,128)(2,1)S(1)}, u32[]{:S(2)}) copy-start(bf16[1,4,256,3200]{3,2,1,0:T(8,128)(2,1)S(1)} %fusion.2) | copy-start | bytes 19660804
  15.3 8.2 %copy-start.6 = (s32[1,4,256]{2,1,0:T(4,128)S(1)}, s32[1,4,256]{2,1,0:T(4,128)}, u32[]{:S(2)}) copy-start(s32[1,4,256]{2,1,0:T(4,128)} %param.13) | copy-start | bytes 12292
  15.3 9.6 %copy-start.2 = (bf16[1,4,128,1408]{3,2,1,0:T(8,128)(2,1)S(1)}, bf16[1,4,128,1408]{3,2,1,0:T(8,128)(2,1)}, u32[]{:S(2)}) copy-start(bf16[1,4,128,1408]{3,2,1,0:T(8,128)(2,1)} %param.12) | copy-start | bytes 4325380
  20.2 80.4 %collective-permute-start.1 = (bf16[1,4,128,3200]{3,2,1,0:T(8,128)(2,1)}, bf16[1,4,128,3200]{3,2,1,0:T(8,128)(2,1)}, u32[]{:S(2)}, u32[]{:S(2)}) collective-permute-start(bf16[1,4,128,3200]{3,2,1,0:T(8,128)(2,1)} %get-tuple-element.12), channel_id=1, source_target_pairs={{0,1},{1,0},{2,3},{3,2},{4,5},{5,4},{6,7},{7,6},{8,9},{9,8},{10,11... | collective-permute-start | bytes 9830408 | tf_op jit(solution)/shard_map/ppermute | solution.py:10
  23.5 85.8 %collective-permute-start = (bf16[1,4,128]{2,1,0:T(4,128)(2,1)S(1)}, bf16[1,4,128]{2,1,0:T(4,128)(2,1)S(1)}, u32[]{:S(2)}, u32[]{:S(2)}) collective-permute-start(bf16[1,4,128]{2,1,0:T(4,128)(2,1)S(1)} %dynamic-slice_bitcast_fusion.1), channel_id=1, source_target_pairs={{0,1},{1,0},{2,3},{3,2},{4,5},{5,4},{6,7},{7,6},{8,9},{9,8},{10,11... | collective-permute-start | bytes 3080 | tf_op jit(solution)/shard_map/ppermute | solution.py:10
  91.1 9.6 %copy-start.7 = (bf16[3200,1408]{1,0:T(8,128)(2,1)S(1)}, bf16[3200,1408]{1,0:T(8,128)(2,1)}, u32[]{:S(2)}) copy-start(bf16[3200,1408]{1,0:T(8,128)(2,1)} %all-gather.4.cloned.1.call-done) | copy-start | bytes 27033604
  108.2 2.6 copy-start.3
  133.6 12.1 %copy-start.4 = (bf16[1,4,3200]{2,1,0:T(4,128)(2,1)S(1)}, bf16[1,4,3200]{2,1,0:T(4,128)(2,1)}, u32[]{:S(2)}) copy-start(bf16[1,4,3200]{2,1,0:T(4,128)(2,1)} %param.11) | copy-start | bytes 76804
  133.7 263.7 %reduce-scatter.7.cloned.1.call-start = ((), (), s32[]{:S(2)}) async-start(), calls=%async_computation.4 | async-start | bytes 2162688
  144.3 182.8 %collective-permute-start.2 = (bf16[1,4,128,3200]{3,2,1,0:T(8,128)(2,1)}, bf16[1,4,128,3200]{3,2,1,0:T(8,128)(2,1)S(1)}, u32[]{:S(2)}, u32[]{:S(2)}) collective-permute-start(bf16[1,4,128,3200]{3,2,1,0:T(8,128)(2,1)} %bitcast.12), channel_id=1, source_target_pairs={{0,1},{1,0},{2,3},{3,2},{4,5},{5,4},{6,7},{7,6},{8,9},{9,8},{10,11... | collective-permute-start | bytes 9830408 | tf_op jit(solution)/shard_map/ppermute | solution.py:10
  327.0 95.8 %all-gather.6.cloned.1.call-start = ((), (), s32[]{:S(2)}) async-start(), calls=%async_computation.3 | async-start | bytes 1843200 | tf_op jit(solution)/shard_map/all_gather | solution.py:106
Sparse Core Ops, SparseCore 0:
  10.1 80.9 all-gather.3
  133.8 190.4 reduce-scatter.8
  327.2 23.7 reduce-scatter.6
  399.7 23.0 all-gather.5
where the time goes:
time: 435 us; the launch traced here: 434 us
  waiting for transfers between devices  249 us (57%)
  matrix products  55.4 us (13%)
  other arithmetic  43.4 us (10%)
  blocking collectives  40.4 us (9%)
  local copies, waits for them, and re-layouts  23.3 us (5%)
  between operations  18.4 us (4%)
  starting transfers between devices  4.93 us (1%)
    unnamed x6, waiting for transfers between devices  172 us
    all_gather x1, waiting for transfers between devices, per_device(): weight = lax.all_gather(mae_weight, 'fsdp', axis=0, tiled=True)  65.8 us
    psum x1, blocking collectives, per_device(): lax.psum((gain_local, loss_local), ('fsdp', 'frame'))  40.4 us
    dot_general x2, matrix products, over_rows(): lax.dot_general(left, right, (((0,), (0,)), ((), ())), preferred_element_...  22.8 us
    convert_element_type x1, other arithmetic, per_device(): (recip * (norm_gain * normed_grad - token_float * recip * recip * inner))...  12 us
    all_gather x1, waiting for transfers between devices, per_device(): shard = lax.all_gather(shard, 'frame', axis=1, tiled=True)  11.2 us
    dot_general x1, matrix products, back_project(): lax.dot_general(grads, weight, (((1,), (1,)), ((), ())), preferred_elemen...  10.6 us
    convert_element_type x1, local copies, waits for them, and re-layouts, per_device(): spread.reshape(samples, frames_here, patches, model_width)  10.4 us
  transfers between devices with their start and end apart: 7, of which 3 were waited for; matrix products, arithmetic and copies ran while one was open for 21% of the time, Pallas kernels for 0%

commit v1 on v0

--- a/solution.py
+++ b/solution.py
@@ -4,6 +4,11 @@
 from jax.sharding import PartitionSpec as P
 
 epsilon = 1e-06
+
+
+def one_after_other(x, first, second):
+    half = lax.psum(x, first)
+    return lax.psum(half, second)
 
 
 def swapped(shard, axis, stride):
@@ -120,7 +125,7 @@
     )
     gain_local = jnp.sum(normed_grad * token_float * recip, axis=(0, 1, 2))
     loss_local = jnp.sum(sample_loss)
-    gain_total, loss_total = lax.psum((gain_local, loss_local), ("fsdp", "frame"))
+    gain_total, loss_total = one_after_other((gain_local, loss_local), "frame", "fsdp")
     frame_count = frames_here * frame_devices
     gain_grad = gain_total / clip_count
     loss = loss_total / (clip_count * frame_count * patches * channels)

time: 435 us -> 459 us (1.055)
  blocking collectives: 40.4 us -> 67.6 us
    psum x1 -> x2, blocking collectives: 40.4 us -> 67.6 us  [the longest x1 57.9 us: one_after_other(): return lax.psum(half, second)]
  transfers between devices with their start and end apart: 7 -> 7, of which waited for: 3 -> 3; matrix products, arithmetic and copies ran while one was open for 21% -> 19% of each run, Pallas kernels for 0% -> 0%
where the time goes in v1:
time: 459 us; the launch traced here: 458 us
  waiting for transfers between devices  246 us (54%)
  blocking collectives  67.6 us (15%)
  matrix products  55.4 us (12%)
  other arithmetic  43 us (9%)
  local copies, waits for them, and re-layouts  23.3 us (5%)
  between operations  18.4 us (4%)
  starting transfers between devices  4.93 us (1%)
    unnamed x6, waiting for transfers between devices  172 us
    all_gather x1, waiting for transfers between devices, per_device(): weight = lax.all_gather(mae_weight, 'fsdp', axis=0, tiled=True)  65.8 us
    psum x1, blocking collectives, one_after_other(): return lax.psum(half, second)  57.9 us
    dot_general x2, matrix products, over_rows(): lax.dot_general(left, right, (((0,), (0,)), ((), ())), preferred_element_...  22.8 us
    convert_element_type x1, other arithmetic, per_device(): (recip * (norm_gain * normed_grad - token_float * recip * recip * inner))...  11.6 us
    dot_general x1, matrix products, back_project(): lax.dot_general(grads, weight, (((1,), (1,)), ((), ())), preferred_elemen...  10.6 us
    convert_element_type x1, local copies, waits for them, and re-layouts, per_device(): spread.reshape(samples, frames_here, patches, model_width)  10.4 us
    psum x1, blocking collectives, one_after_other(): half = lax.psum(x, first)  9.72 us
  transfers between devices with their start and end apart: 7, of which 3 were waited for; matrix products, arithmetic and copies ran while one was open for 19% of the time, Pallas kernels for 0%

profile of v1, /device:TPU:0, one launch (start us, length us, event | category | flops | bytes accessed | tf_op | source)
XLA Modules:
  0.0 458.4 jit_solution(3298181236001652921)
XLA Ops:
  8.0 4.4 fusion.7
  12.7 2.6 fusion.2
  15.3 3.2 dynamic-slice_bitcast_fusion
  18.6 1.7 copy-done.1
  20.2 3.2 collective-permute-start.1
  25.3 65.8 %all-gather.4.cloned.1.call-done = bf16[3200,1408]{1,0:T(8,128)(2,1)} async-done(((bf16[200,1408]{1,0:T(8,128)(2,1)}), bf16[3200,1408]{1,0:T(8,128)(2,1)}) %all-gather.4.cloned.1.call-update) | async-done | bytes 9011216 | tf_op jit(solution)/shard_map/all_gather | solution.py:57
  91.1 9.5 %fusion.26 = f32[512,1408]{1,0:T(8,128)S(1)} fusion(bf16[512,3200]{1,0:T(8,128)(2,1)} %bitcast.116, bf16[3200,1408]{1,0:T(8,128)(2,1)} %all-gather.4.cloned.1.call-done), kind=kOutput, calls=%fused_computation.71 | convolution fusion | flops 4613734400 | bytes 15171584 | tf_op jit(solution)/shard_map/dot_general | solution.py:90
  100.7 7.5 %multiply_reduce_fusion.3 = (f32[512]{0:T(512)S(1)}, f32[512,1408]{1,0:T(8,128)S(1)}) fusion(f32[512,1408]{1,0:T(8,128)S(1)} %fusion.26, bf16[512,3200]{1,0:T(8,128)(2,1)} %bitcast.8, bf16[3200,1408]{1,0:T(8,128)(2,1)S(1)} %copy-done.7), kind=kOutput, calls=%fused_computation.31 | convolution fusion | flops 4616617472 | bytes 18057216 | tf_op jit(solution)/shard_map/dot_general | solution.py:91
  110.8 9.1 %fusion.27 = f32[3200,1408]{1,0:T(8,128)} fusion(bf16[512,3200]{1,0:T(8,128)(2,1)S(1)} %bitcast.117, bf16[512,1408]{1,0:T(8,128)(2,1)S(1)} %multiply_convert_fusion), kind=kOutput, calls=%fused_computation.72 | convolution fusion | flops 4613734400 | bytes 22740992 | tf_op jit(solution)/shard_map/dot_general | solution.py:28
  119.9 13.7 %add_multiply_fusion = f32[3200,1408]{1,0:T(8,128)} fusion(f32[3200,1408]{1,0:T(8,128)} %fusion.27, bf16[512,3200]{1,0:T(8,128)(2,1)} %bitcast.8, bf16[512,1408]{1,0:T(8,128)(2,1)S(1)} %multiply_convert_fusion), kind=kOutput, calls=%fused_computation.4 | convolution fusion | flops 4622745600 | bytes 40763392 | tf_op jit(solution)/shard_map/dot_general | solution.py:28
  133.7 10.6 %fusion.14 = bf16[512,3200]{1,0:T(8,128)(2,1)} fusion(bf16[512,1408]{1,0:T(8,128)(2,1)S(1)} %multiply_convert_fusion, bf16[3200,1408]{1,0:T(8,128)(2,1)} %all-gather.4.cloned.1.call-done), kind=kOutput, calls=%fused_computation.22 | convolution fusion | flops 4617011200 | bytes 13729792 | tf_op jit(solution)/shard_map/dot_general | solution.py:36
  144.3 1.5 collective-permute-start.2
  145.9 5.0 %fusion.12 = f32[4,1,3200]{2,1,0:T(1,128)S(1)} fusion(bf16[1,4,256,3200]{3,2,1,0:T(8,128)(2,1)} %copy-done.1, bf16[4,256,1]{1,0,2:T(4,128)(2,1)S(1)} %get-tuple-element.17), kind=kOutput, calls=%fused_computation.20 | convolution fusion | flops 6553600 | bytes 6606848 | tf_op jit(solution)/shard_map/bfp,bfpd->bfd/dot_general | solution.py:63
  153.3 170.9 %reduce-scatter.9.cloned.1.call-done = f32[200,1408]{1,0:T(8,128)} async-done(((f32[3200,1408]{1,0:T(8,128)}), f32[200,1408]{1,0:T(8,128)}) %reduce-scatter.9.cloned.1.call-update) | async-done | bytes 1126416
  324.2 2.8 copy.19
  327.1 8.7 %fusion.11 = f32[1,4,2,128,3200]{4,3,1,2,0:T(8,128)} fusion(bf16[1,4,1,128,3200]{4,3,1,2,0:T(8,128)(2,1)S(1)} %bitcast.118, bf16[1,4,1,128,3200]{4,3,1,2,0:T(8,128)(2,1)} %bitcast.11, pred[]{:T(512)S(6)} %eq.3), kind=kLoop, calls=%fused_computation.19 | loop fusion | flops 13107200 | bytes 19660800 | tf_op jit(solution)/shard_map/convert_element_type | solution.py:119
  335.8 10.4 %copy.15 = f32[1,4,2,128,3200]{4,3,2,1,0:T(8,128)} copy(f32[1,4,2,128,3200]{4,3,1,2,0:T(8,128)} %fusion.11) | data formatting | bytes 26214400 | tf_op jit(solution)/shard_map/convert_element_type | solution.py:119
  346.2 9.5 %fusion.10 = (f32[3200]{0:T(1024)S(1)}, f32[4,256]{1,0:T(4,128)S(1)}) fusion(bf16[1,4,256,3200]{3,2,1,0:T(8,128)(2,1)} %param.8, f32[1,4,2,128,3200]{4,3,2,1,0:T(8,128)} %copy.15, f32[4,3200]{1,0:T(4,128)S(1)} %fusion.20, f32[4,256]{1,0:T(4,128)S(1)} %get-tuple-element.16, f32[4,256]{1,0:T(4,128)S(1)} %add_rsqrt_fusion, f32[3200]{0:T(1024)S(1)} %copy-done.5), kind=kLoop, calls=%fused_computation.15 | loop fusion | flops 32763776 | bytes 19749888 | tf_op jit(solution)/shard_map/reduce_sum | solution.py:126
  355.7 9.7 %all-reduce.2 = (f32[3200]{0:T(1024)S(1)}, f32[]{:T(128)}) all-reduce(f32[3200]{0:T(1024)S(1)} %get-tuple-element.4, f32[]{:T(128)} %bitcast.30), channel_id=1, replica_groups=mesh['fsdp'=16,'frame'=2] {'frame'}, use_global_device_ids=true, to_apply=%region_11.12 | all-reduce | flops 3201 | bytes 25608 | tf_op jit(solution)/shard_map/psum | solution.py:10
  365.4 57.9 %all-reduce.1 = (f32[3200]{0:T(1024)S(1)}, f32[]{:T(128)}) all-reduce(f32[3200]{0:T(1024)S(1)} %get-tuple-element.12, f32[]{:T(128)} %get-tuple-element.13), channel_id=1, replica_groups=mesh['fsdp'=16,'frame'=2] {'fsdp'}, use_global_device_ids=true, to_apply=%region_12.13 | all-reduce | flops 3201 | bytes 25608 | tf_op jit(solution)/shard_map/psum | solution.py:11
  424.6 2.2 copy.20
  426.8 11.6 %fusion.6 = bf16[1,4,256,3200]{3,2,1,0:T(8,128)(2,1)} fusion(bf16[1,4,256,3200]{3,2,1,0:T(8,128)(2,1)} %param.8, f32[1,4,2,128,3200]{4,3,2,1,0:T(8,128)} %copy.15, f32[4,256]{1,0:T(4,128)S(1)} %broadcast_multiply_fusion.2, f32[4,3200]{1,0:T(4,128)S(1)} %fusion.20, f32[4,256]{1,0:T(4,128)S(1)} %get-tuple-element.16, f32[3200]{0:T(1024)S(1)} %copy-done.5, ...), kind=kLoop, calls=%fused_computation.11 | loop fusion | flops 36044800 | bytes 26290688 | tf_op jit(solution)/shard_map/convert_element_type | solution.py:123
  438.4 8.3 %all-gather.6.cloned.1.call-done = f32[2,704,200]{1,2,0:T(8,128)} async-done(((f32[1,704,200]{1,2,0:T(8,128)}), f32[2,704,200]{1,2,0:T(8,128)}) %all-gather.6.cloned.1.call-update) | async-done | bytes 1126416 | tf_op jit(solution)/shard_map/all_gather | solution.py:111
  448.7 2.0 reshape.268
  (50 shorter events, 8.2 us)
Async XLA Ops:
  7.2 5.2 %copy-start.5 = (f32[3200]{0:T(1024)S(1)}, f32[3200]{0:T(1024)}, u32[]{:S(2)}) copy-start(f32[3200]{0:T(1024)} %param.9) | copy-start | bytes 38404
  7.2 83.9 %all-gather.4.cloned.1.call-start = ((), (), s32[]{:S(2)}) async-start(), calls=%async_computation.2 | async-start | bytes 9574400 | tf_op jit(solution)/shard_map/all_gather | solution.py:57
  7.9 316.3 %reduce-scatter.9.cloned.1.call-start = ((), (), s32[]{:S(2)}) async-start(), calls=%async_computation.5 | async-start | bytes 19148800
  8.0 4.7 %copy-start = (bf16[1,4,256,3200]{3,2,1,0:T(8,128)(2,1)S(1)}, bf16[1,4,256,3200]{3,2,1,0:T(8,128)(2,1)}, u32[]{:S(2)}) copy-start(bf16[1,4,256,3200]{3,2,1,0:T(8,128)(2,1)} %param.8) | copy-start | bytes 19660804
  15.3 4.9 %copy-start.1 = (bf16[1,4,256,3200]{3,2,1,0:T(8,128)(2,1)}, bf16[1,4,256,3200]{3,2,1,0:T(8,128)(2,1)S(1)}, u32[]{:S(2)}) copy-start(bf16[1,4,256,3200]{3,2,1,0:T(8,128)(2,1)S(1)} %fusion.2) | copy-start | bytes 19660804
  15.3 8.2 %copy-start.6 = (s32[1,4,256]{2,1,0:T(4,128)S(1)}, s32[1,4,256]{2,1,0:T(4,128)}, u32[]{:S(2)}) copy-start(s32[1,4,256]{2,1,0:T(4,128)} %param.13) | copy-start | bytes 12292
  15.3 9.6 %copy-start.2 = (bf16[1,4,128,1408]{3,2,1,0:T(8,128)(2,1)S(1)}, bf16[1,4,128,1408]{3,2,1,0:T(8,128)(2,1)}, u32[]{:S(2)}) copy-start(bf16[1,4,128,1408]{3,2,1,0:T(8,128)(2,1)} %param.12) | copy-start | bytes 4325380
  20.2 80.4 %collective-permute-start.1 = (bf16[1,4,128,3200]{3,2,1,0:T(8,128)(2,1)}, bf16[1,4,128,3200]{3,2,1,0:T(8,128)(2,1)}, u32[]{:S(2)}, u32[]{:S(2)}) collective-permute-start(bf16[1,4,128,3200]{3,2,1,0:T(8,128)(2,1)} %get-tuple-element.14), channel_id=1, source_target_pairs={{0,1},{1,0},{2,3},{3,2},{4,5},{5,4},{6,7},{7,6},{8,9},{9,8},{10,11... | collective-permute-start | bytes 9830408 | tf_op jit(solution)/shard_map/ppermute | solution.py:15
  23.5 85.8 %collective-permute-start = (bf16[1,4,128]{2,1,0:T(4,128)(2,1)S(1)}, bf16[1,4,128]{2,1,0:T(4,128)(2,1)S(1)}, u32[]{:S(2)}, u32[]{:S(2)}) collective-permute-start(bf16[1,4,128]{2,1,0:T(4,128)(2,1)S(1)} %dynamic-slice_bitcast_fusion.1), channel_id=1, source_target_pairs={{0,1},{1,0},{2,3},{3,2},{4,5},{5,4},{6,7},{7,6},{8,9},{9,8},{10,11... | collective-permute-start | bytes 3080 | tf_op jit(solution)/shard_map/ppermute | solution.py:15
  91.1 9.6 %copy-start.7 = (bf16[3200,1408]{1,0:T(8,128)(2,1)S(1)}, bf16[3200,1408]{1,0:T(8,128)(2,1)}, u32[]{:S(2)}) copy-start(bf16[3200,1408]{1,0:T(8,128)(2,1)} %all-gather.4.cloned.1.call-done) | copy-start | bytes 27033604
  108.2 2.6 copy-start.3
  133.6 12.1 %copy-start.4 = (bf16[1,4,3200]{2,1,0:T(4,128)(2,1)S(1)}, bf16[1,4,3200]{2,1,0:T(4,128)(2,1)}, u32[]{:S(2)}) copy-start(bf16[1,4,3200]{2,1,0:T(4,128)(2,1)} %param.11) | copy-start | bytes 76804
  133.7 290.9 %reduce-scatter.7.cloned.1.call-start = ((), (), s32[]{:S(2)}) async-start(), calls=%async_computation.4 | async-start | bytes 2162688
  144.3 182.8 %collective-permute-start.2 = (bf16[1,4,128,3200]{3,2,1,0:T(8,128)(2,1)}, bf16[1,4,128,3200]{3,2,1,0:T(8,128)(2,1)S(1)}, u32[]{:S(2)}, u32[]{:S(2)}) collective-permute-start(bf16[1,4,128,3200]{3,2,1,0:T(8,128)(2,1)} %bitcast.12), channel_id=1, source_target_pairs={{0,1},{1,0},{2,3},{3,2},{4,5},{5,4},{6,7},{7,6},{8,9},{9,8},{10,11... | collective-permute-start | bytes 9830408 | tf_op jit(solution)/shard_map/ppermute | solution.py:15
  327.0 119.6 %all-gather.6.cloned.1.call-start = ((), (), s32[]{:S(2)}) async-start(), calls=%async_computation.3 | async-start | bytes 1843200 | tf_op jit(solution)/shard_map/all_gather | solution.py:111
Sparse Core Ops, SparseCore 0:
  10.1 80.9 all-gather.3
  133.8 190.4 reduce-scatter.8
  327.2 23.7 reduce-scatter.6
  426.9 19.7 all-gather.5
